TPU v7x, 1024 devices: a whole 8x8x8 slice. The times are simulated.
1024 devices in a mesh: dp: 128 (over x, y, core), group: 8 (over z).
Axes of the slice: x: 8, y: 8, z: 8, core: 2. Of those that a mesh axis runs over, the one named last changes fastest.
Arguments:
- features: bfloat16 [128, 8, 256, 1536], P('dp', 'group'), may hold values from -6 to 6
- cotangent: bfloat16 [128, 8, 256, 1536], P('dp', 'group'), may hold values from -24 to 24
- lengths: int32 [128, 8, 4], P('dp', 'group'), may hold values from 1 to 128, 256 in all within a row
- destination: int32 [128, 8, 2], P('dp', 'group'), may hold values from 0 to 1, as said below
- kernel: float32 [31, 1536], replicated, may hold values from -1 to 1
- norm_gain: float32 [1536], replicated, may hold values from 0.1 to 1.9
- norm_bias: float32 [1536], replicated, may hold values from -3 to 3
Outputs:
- input_grad: bfloat16 [128, 8, 256, 1536], P('dp', 'group')
- kernel_grad: float32 [31, 1536], P(None, 'dp')
- norm_grad: float32 [2, 1536], P(None, 'dp')
Inputs may be any that keep to these rules, and one draw needn't show every extreme that they name: Each device's lengths sum to 256, and the longest is exactly half of 256. `destination`: exactly 1 of each device's 2 blocks are marked 1.
All inputs are finite; a program needn't handle non-finite values.
Results may differ from a plain program's by a relative error of at most 0.001.
Values may be sent and summed in bfloat16 or wider, within the bound.
A program may use at most 32 MiB of HBM per device.

v0:
```python
import jax
import jax.numpy as jnp
from jax import lax
from jax.sharding import PartitionSpec as P

BLK = 128
MOVE = 1


EPSILON = 1e-05


def from_behind(block, axis, distance):
    devices = range(lax.axis_size(axis))
    route = [((i - distance) % len(devices), i) for i in devices]
    return lax.ppermute(block, axis, route)


def forward_pass(features, cotangent, lengths, kernel, norm_gain, norm_bias):
    frames = features.shape[0]
    tap_count = kernel.shape[0]
    half_span = tap_count // 2
    utt_ends = jnp.cumsum(lengths)
    starts = utt_ends - lengths
    position = jnp.arange(frames, dtype=jnp.int32)
    inside = (position[:, None] >= starts[None, :]) & (position[:, None] < utt_ends[None, :])
    utt_start = jnp.sum(jnp.where(inside, starts[None, :], 0), axis=1)
    utt_end = jnp.sum(jnp.where(inside, utt_ends[None, :], 0), axis=1)
    source = features.astype(jnp.float32)
    padded = jnp.pad(source, ((half_span, half_span), (0, 0)))
    inside_masks = []
    mixed_conv = jnp.zeros_like(source)
    for tap_index in range(tap_count):
        target = position + (tap_index - half_span)
        inside_mask = ((target >= utt_start) & (target < utt_end)).astype(jnp.float32)[:, None]
        inside_masks.append(inside_mask)
        mixed_conv = (
            mixed_conv + kernel[tap_index] * padded[tap_index : tap_index + frames] * inside_mask
        )
    row_mean = jnp.mean(mixed_conv, axis=1, keepdims=True)
    centred = mixed_conv - row_mean
    variance = jnp.mean(centred * centred, axis=1, keepdims=True)
    inv_scale = lax.rsqrt(variance + EPSILON)
    normed = centred * inv_scale
    activation = normed * norm_gain + norm_bias
    sigmoid_act = jax.nn.sigmoid(activation)
    dact = cotangent.astype(jnp.float32) * sigmoid_act * (1.0 + activation * (1.0 - sigmoid_act))
    dnorm = dact * norm_gain
    dconv = inv_scale * (
        dnorm
        - jnp.mean(dnorm, axis=1, keepdims=True)
        - normed * jnp.mean(dnorm * normed, axis=1, keepdims=True)
    )
    return (padded, inside_masks, normed, dact, dconv)


def grad_rows(dconv, inside_masks, kernel, start, rows):
    tap_count = kernel.shape[0]
    half_span = tap_count // 2
    dconv_pad = jnp.pad(dconv, ((half_span, half_span), (0, 0)))
    total = jnp.zeros((rows, dconv.shape[1]), jnp.float32)
    for tap_index in range(tap_count):
        mask_pad = jnp.pad(inside_masks[tap_index], ((half_span, half_span), (0, 0)))
        offset = start + 2 * half_span - tap_index
        piece = lax.dynamic_slice_in_dim(dconv_pad, offset, rows, 0) * lax.dynamic_slice_in_dim(
            mask_pad, offset, rows, 0
        )
        total = total + kernel[tap_index] * piece
    return total.astype(jnp.bfloat16)


def param_terms(padded, inside_masks, normed, dact, dconv, kernel):
    frames = dconv.shape[0]
    kernel_rows = []
    for tap_index in range(kernel.shape[0]):
        weighted = dconv * inside_masks[tap_index]
        kernel_rows.append(jnp.sum(weighted * padded[tap_index : tap_index + frames], axis=0))
    kernel_term = jnp.stack(kernel_rows, axis=0)
    norm_term = jnp.stack([jnp.sum(dact * normed, axis=0), jnp.sum(dact, axis=0)], axis=0)
    return (kernel_term, norm_term)


def local(features, cotangent, lengths, destination, kernel, norm_gain, norm_bias):
    frames = features.shape[2]
    channels = features.shape[3]
    padded, inside_masks, normed, dact, dconv = forward_pass(
        features[0, 0], cotangent[0, 0], lengths[0, 0], kernel, norm_gain, norm_bias
    )
    block_count = frames // BLK
    block_order = jnp.argsort(
        destination[0, 0] * block_count + jnp.arange(block_count, dtype=jnp.int32)
    )
    local_grad = grad_rows(dconv, inside_masks, kernel, 0, frames)
    blocks = local_grad.reshape(block_count, BLK, channels)
    sorted_blocks = blocks[block_order]
    staying = sorted_blocks[: block_count - MOVE]
    movers = from_behind(sorted_blocks[block_count - MOVE :], "dp", 1)
    kernel_term, norm_term = param_terms(padded, inside_masks, normed, dact, dconv, kernel)
    input_grad = jnp.concatenate([staying, movers], axis=0).reshape(1, 1, frames, channels)
    whole_sums = lax.psum((kernel_term, norm_term), "group")
    kernel_share, norm_share = (
        lax.psum_scatter(whole_sums[0], "dp", scatter_dimension=1, tiled=True),
        lax.psum_scatter(whole_sums[1], "dp", scatter_dimension=1, tiled=True),
    )
    device_count = lax.axis_size("dp") * lax.axis_size("group")
    grad_scale = 1.0 / jnp.sqrt(jnp.float32(device_count * frames))
    return (input_grad, kernel_share * grad_scale, norm_share * grad_scale)


def solution(mesh):
    return jax.shard_map(
        local,
        mesh=mesh,
        in_specs=(
            P("dp", "group", None, None),
            P("dp", "group", None, None),
            P("dp", "group", None),
            P("dp", "group", None),
            P(),
            P(),
            P(),
        ),
        out_specs=(P("dp", "group", None, None), P(None, "dp"), P(None, "dp")),
        check_vma=False,
    )
```

profile of v0, /device:TPU:1, one launch (start us, length us, event | category | flops | bytes accessed | tf_op | source)
XLA Modules:
  0.0 598.0 jit_solution(17749173005262516352)
XLA Ops:
  7.2 0.0 all-reduce.37.cloned.1.call-start
  7.2 1.9 slice_reduce_fusion.30
  9.1 1.5 slice_reduce_fusion.29
  10.6 0.8 reduce-window.7
  11.4 0.7 bitcast_subtract_fusion
  12.1 1.3 bitcast_convert_fusion
  13.4 0.1 select_reduce_fusion.1
  13.5 12.4 %fusion.124 = (f32[256]{0:T(256)S(1)}, f32[256,1536]{1,0:T(8,128)S(1)}) fusion(f32[256]{0:T(256)S(1)} %get-tuple-element.121, f32[1536]{0:T(1024)S(1)} %get-tuple-element.78, f32[256]{0:T(256)S(1)} %get-tuple-element.122, f32[1536]{0:T(1024)S(1)} %get-tuple-element.79, f32[256]{0:T(256)S(1)} %get-tuple-element.123, f32[1536]{0:T(1024)S(1)} %get-tuple-element.50, ...), kind=kLoop, calls=%fused_computation.364 | loop fusion | flops 36568832 | bytes 3368960 | tf_op jit(solution)/shard_map/reduce_sum | solution.py:40
  26.0 0.0 copy-start.2
  26.0 0.0 copy-start.3
  26.0 0.3 multiply_reduce_fusion.33
  26.3 0.8 copy-done.1
  27.1 1.4 multiply_reduce_fusion
  28.5 4.0 multiply_reduce_fusion.1
  32.6 3.5 multiply_reduce_fusion.20
  36.1 3.6 multiply_reduce_fusion.10
  39.8 1.3 multiply_reduce_fusion.29
  41.5 2.8 stack.136
  44.3 0.0 all-reduce.37.cloned.1.call-update
  44.4 0.6 sort.17
  45.0 0.1 compare_and_fusion.29
  45.1 0.1 fusion.93
  45.1 0.1 fusion.95
  45.2 0.1 fusion.97
  45.3 0.1 fusion.99
  45.4 0.1 fusion.101
  45.4 0.1 fusion.103
  45.5 0.1 fusion.105
  45.6 0.1 fusion.107
  45.7 0.1 fusion.109
  45.7 0.1 fusion.111
  45.8 0.1 fusion.113
  45.9 0.1 fusion.115
  46.0 0.1 fusion.117
  46.0 0.1 fusion.119
  46.1 0.1 fusion.121
  46.2 9.5 %fusion.76 = bf16[256,1536]{1,0:T(8,128)(2,1)S(1)} fusion(f32[256,1536]{1,0:T(8,128)S(1)} %get-tuple-element.84, f32[256]{0:T(256)S(1)} %bitcast.88, f32[256]{0:T(256)S(1)} %bitcast.87, f32[256]{0:T(256)S(1)} %bitcast.86, f32[256]{0:T(256)S(1)} %bitcast.85, f32[256]{0:T(256)S(1)} %bitcast.84, f32[256]{0:T(256)S(1)} %bitcast.83, f32[256]{0:T(256)S(1)} %bitcast.82, ...), kind=kLoop, calls=%fused_computation.137 | loop fusion | flops 36569088 | bytes 2581504 | tf_op jit(solution)/shard_map/convert_element_type | solution.py:69
  55.7 0.6 gather_fusion
  56.3 0.1 fusion.125
  56.4 4.7 collective-permute-start
  61.1 501.7 %all-reduce.33 = f32[2,1536]{1,0:T(2,128)S(1)} all-reduce(f32[2,1536]{1,0:T(2,128)S(1)} %pad_maximum_fusion.1), channel_id=3, replica_groups=mesh['dp'=128,'group'=8] {'dp'}, use_global_device_ids=true, to_apply=%region_44.45.clone | all-reduce | flops 3072 | bytes 24576
  562.8 1.3 dynamic-slice
  564.7 0.1 constant_dynamic-slice_fusion
  564.8 0.8 constant_dynamic-slice_fusion.1
  565.6 23.3 %all-reduce.34 = (f32[31,12]{1,0:T(8,128)S(1)}, f32[2,12]{1,0:T(2,128)S(1)}) all-reduce(f32[31,12]{1,0:T(8,128)S(1)} %constant_dynamic-slice_fusion.1, f32[2,12]{1,0:T(2,128)S(1)} %constant_dynamic-slice_fusion), channel_id=1, replica_groups=mesh['dp'=128,'group'=8] {'group'}, use_global_device_ids=true, to_apply=%region_39.40 | all-reduce | flops 396 | bytes 3168 | tf_op jit(solution)/shard_map/psum | solution.py:100
  589.0 0.7 copy.12
  589.6 0.6 broadcast_multiply_fusion.1
  590.2 0.9 pad_maximum_fusion
  (52 shorter events, 0.3 us)
Async XLA Ops:
  7.2 557.6 %all-reduce.37.cloned.1.call-start = ((), (), s32[]{:S(2)}) async-start(), calls=%async_computation | async-start | bytes 393216
  26.0 1.1 copy-start.1
  26.0 1.1 copy-start.2
  26.0 1.1 copy-start.3
  36.1 3.7 copy-start
  39.8 4.6 copy-start.4
  56.4 533.8 %collective-permute-start = (bf16[1,128,1536]{2,1,0:T(8,128)(2,1)S(1)}, bf16[1,128,1536]{2,1,0:T(8,128)(2,1)S(1)}, u32[]{:S(2)}, u32[]{:S(2)}) collective-permute-start(bf16[1,128,1536]{2,1,0:T(8,128)(2,1)S(1)} %get-tuple-element.89), channel_id=1, source_target_pairs={{1016,0},{0,8},{8,16},{16,24},{24,32},{32,40},{40,48},{48,56},{56,... | collective-permute-start | bytes 1179656 | tf_op jit(solution)/shard_map/ppermute | solution.py:16
Sparse Core Ops, SparseCore 0:
  44.5 211.4 all-reduce.36
where the time goes:
time: 609 us; the launch traced here: 598 us
  blocking collectives  525 us (86%)
  other arithmetic  42.4 us (7%)
  between operations  15.2 us (2%)
  local copies, waits for them, and re-layouts  10.7 us (2%)
    unnamed x1, blocking collectives  502 us
    psum x1, blocking collectives, local(): whole_sums = lax.psum((kernel_term, norm_term), 'group')  23.3 us
    reduce_sum x4, other arithmetic, param_terms(): jnp.sum(weighted * padded[tap_index:tap_index + frames], axis=0)  12.5 us
    reduce_sum x1, other arithmetic, forward_pass(): row_mean = jnp.mean(mixed_conv, axis=1, keepdims=True)  12.4 us
  transfers between devices with their start and end apart: 2, of which 0 were waited for; matrix products, arithmetic and copies ran while one was open for 3% of the time, Pallas kernels for 0%

commit v1 on v0

v1 whole, which is shorter than its diff:
```python
import math

import jax
import jax.numpy as jnp
from jax import lax
from jax.experimental import pallas as pl
from jax.experimental.pallas import tpu as pltpu
from jax.sharding import PartitionSpec as P

EPSILON = 1e-05
GAP = 16
LANES = 128
KEEP = 40
TILE = 8
CORES = 2
MESH = pl.DeviceIdType.MESH


def tap_groups(taps):
    return [[k for k in range(phase, taps, TILE)] for phase in range(TILE)]


def convolve(source, row, weights, taps, rows):
    total = None
    for group in tap_groups(taps):
        window = source[pl.ds(row + group[0], rows + TILE * (len(group) - 1)), :]
        for step, tap in enumerate(group):
            term = weights(tap) * window[TILE * step : TILE * step + rows]
            total = term if total is None else total + term
    return total


def local_kernel(
    lengths, destination, features, cotangent, kernel, gain, bias,
    grad_out, packed_out,
    stage, padded, conv, dnorm, dconv, owner, row_a, row_b, mean, scale, tap_sums, terms, columnwise,
):
    frames, channels = features.shape
    utterances = lengths.shape[0]
    taps = kernel.shape[0]
    half_span = taps // 2
    blocks = channels // LANES
    spread = frames + GAP * (utterances - 1)
    margin = GAP * (utterances - 1)
    chunk = spread // 2
    inverse = 1.0 / channels

    place = lax.broadcasted_iota(jnp.int32, (spread, LANES), 0)
    wide_owner = jnp.full((spread, LANES), -1, jnp.int32)
    begin = 0
    for u in range(utterances):
        finish = begin + lengths[u]
        here = (place >= begin + GAP * u) & (place < finish + GAP * u)
        wide_owner = jnp.where(here, u, wide_owner)
        begin = finish
    owner[...] = wide_owner

    edge = jnp.zeros((GAP, LANES), jnp.float32)
    terms[...] = jnp.zeros_like(terms)

    def spread_rows(value):
        stage[pl.ds(margin, frames), :] = value
        ids = owner[...]
        out = jnp.zeros((spread, LANES), jnp.float32)
        for u in range(utterances):
            out = jnp.where(ids == u, stage[pl.ds(margin - GAP * u, spread), :], out)
        return out

    def columns(b):
        return pl.ds(pl.multiple_of(b * LANES, LANES), LANES)

    def row_total(ref):
        return jnp.broadcast_to(jnp.sum(ref[...], axis=1, keepdims=True), (spread, LANES))

    stage[...] = jnp.zeros_like(stage)
    row_a[...] = jnp.zeros_like(row_a)

    @pl.loop(0, blocks)
    def _(b):
        padded[b, pl.ds(0, GAP), :] = edge
        padded[b, pl.ds(GAP + spread, GAP), :] = edge
        padded[b, pl.ds(GAP, spread), :] = spread_rows(features[:, columns(b)].astype(jnp.float32))
        for c in range(2):
            value = convolve(
                padded.at[b], GAP - half_span + chunk * c,
                lambda tap: kernel[pl.ds(tap, 1), columns(b)], taps, chunk,
            )
            conv[b, pl.ds(chunk * c, chunk), :] = value
            row_a[pl.ds(chunk * c, chunk), :] += value

    mean[...] = row_total(row_a) * inverse
    row_a[...] = jnp.zeros_like(row_a)

    @pl.loop(0, blocks)
    def _(b):
        centred = conv[b] - mean[...]
        conv[b] = centred
        row_a[...] += centred * centred

    scale[...] = lax.rsqrt(row_total(row_a) * inverse + EPSILON)
    row_a[...] = jnp.zeros_like(row_a)
    row_b[...] = jnp.zeros_like(row_b)

    @pl.loop(0, blocks)
    def _(b):
        normed = conv[b] * scale[...]
        conv[b] = normed
        g = gain[:, columns(b)]
        act = normed * g + bias[:, columns(b)]
        gate = jax.nn.sigmoid(act)
        dact = spread_rows(cotangent[:, columns(b)].astype(jnp.float32)) * gate * (1.0 + act * (1.0 - gate))
        terms[pl.ds(taps, 1), columns(b)] = jnp.sum(dact * normed, axis=0, keepdims=True)
        terms[pl.ds(taps + 1, 1), columns(b)] = jnp.sum(dact, axis=0, keepdims=True)
        weighted = dact * g
        dnorm[b] = weighted
        row_a[...] += weighted
        row_b[...] += weighted * normed

    mean[...] = row_total(row_a) * inverse
    row_b[...] = row_total(row_b) * inverse

    @pl.loop(0, blocks)
    def _(b):
        dconv[b, pl.ds(0, GAP), :] = edge
        dconv[b, pl.ds(GAP + spread, GAP), :] = edge
        dconv[b, pl.ds(GAP, spread), :] = scale[...] * (dnorm[b] - mean[...] - conv[b] * row_b[...])
        for c in range(2):
            ours = dconv[b, pl.ds(GAP + chunk * c, chunk), :]
            for group in tap_groups(taps):
                window = padded[
                    b, pl.ds(GAP - half_span + chunk * c + group[0], chunk + TILE * (len(group) - 1)), :
                ]
                for step, tap in enumerate(group):
                    product = ours * window[TILE * step : TILE * step + chunk]
                    part = jnp.sum(product.reshape(chunk // TILE, TILE, LANES), axis=0)
                    tap_sums[tap] = part if c == 0 else tap_sums[tap] + part
        terms[pl.ds(0, taps), columns(b)] = jnp.sum(tap_sums[...], axis=1)
        square = jnp.concatenate([terms[:, columns(b)], jnp.zeros((LANES - KEEP, LANES), jnp.float32)], axis=0)
        columnwise[columns(b), :] = square.T

    halves, lines, share = packed_out.shape[:3]
    depth = channels // (halves * lines * share)

    @pl.loop(0, lines)
    def _(x):
        for y in range(halves * share):
            first = (x * halves * share + y) * depth
            tile = None
            for a in range(depth // TILE):
                piece = columnwise[pl.ds(pl.multiple_of(first + TILE * a, TILE), TILE), :]
                piece = piece if a == 0 else pltpu.roll(piece, KEEP * a, 1)
                tile = piece if tile is None else tile + piece
            packed_out[y // share, x, y % share] = tile

    @pl.loop(0, blocks)
    def _(b):
        for c in range(2):
            stage[pl.ds(chunk * c, chunk), :] = convolve(
                dconv.at[b], GAP - half_span + chunk * c,
                lambda tap: kernel[pl.ds(taps - 1 - tap, 1), columns(b)], taps, chunk,
            )
        spot = lax.broadcasted_iota(jnp.int32, (frames, LANES), 0)
        grad = stage[pl.ds(0, frames), :]
        begin = lengths[0]
        for u in range(1, utterances):
            grad = jnp.where(spot >= begin, stage[pl.ds(GAP * u, frames), :], grad)
            begin = begin + lengths[u]
        grad = grad.astype(grad_out.dtype)
        size = grad_out.shape[1]
        for i in range(frames // size):
            grad_out[destination[i], :, columns(b)] = grad[size * i : size * (i + 1)]


def local_pass(features, cotangent, lengths, destination, kernel, gain, bias, side=8):
    frames, channels = features.shape
    utterances = lengths.shape[0]
    taps = kernel.shape[0]
    size = frames // destination.shape[0]
    blocks = channels // LANES
    spread = frames + GAP * (utterances - 1)
    margin = GAP * (utterances - 1)
    smem = pl.BlockSpec(memory_space=pltpu.SMEM)
    vmem = pl.BlockSpec(memory_space=pltpu.VMEM)
    f32 = jnp.float32
    return pl.pallas_call(
        local_kernel,
        out_shape=(
            jax.ShapeDtypeStruct((2, size, channels), jnp.bfloat16),
            jax.ShapeDtypeStruct((CORES, side, side // CORES, TILE, LANES), f32),
        ),
        in_specs=[smem, smem] + [vmem] * 5,
        out_specs=[vmem, vmem],
        scratch_shapes=[
            pltpu.VMEM((margin + spread, LANES), f32),
            pltpu.VMEM((blocks, spread + 2 * GAP, LANES), f32),
            pltpu.VMEM((blocks, spread, LANES), f32),
            pltpu.VMEM((blocks, spread, LANES), f32),
            pltpu.VMEM((blocks, spread + 2 * GAP, LANES), f32),
            pltpu.VMEM((spread, LANES), jnp.int32),
            pltpu.VMEM((spread, LANES), f32),
            pltpu.VMEM((spread, LANES), f32),
            pltpu.VMEM((spread, LANES), f32),
            pltpu.VMEM((spread, LANES), f32),
            pltpu.VMEM((taps, TILE, LANES), f32),
            pltpu.VMEM((KEEP, channels), f32),
            pltpu.VMEM((channels, LANES), f32),
        ],
        name="conv_block",
    )(lengths, destination, features, cotangent, kernel, gain[None], bias[None])


def share_kernel(
    side, depth_z, divisor,
    grads, packed,
    grad_out, kernel_out, norm_out,
    from_core, sum_core, from_x, sum_x, from_y, sum_y, from_z,
    core_sent, core_got, x_sent, x_got, y_sent, y_got, z_sent, z_got, move_sent, move_got, stay_done,
):
    me = lax.axis_index("dp")
    z = lax.axis_index("group")
    ring = side * side * CORES
    core = lax.rem(me, CORES)
    chip = lax.div(me, CORES)
    y = lax.rem(chip, side)
    x = lax.div(chip, side)
    share = side // CORES

    def at(x, y, core):
        return ((x * side + y) * CORES + core, z)

    partner = at(x, y, 1 - core)
    following = (lax.rem(me + 1, ring), z)
    beside = (lax.rem(me + ring + 2 * core - 1, ring), z)
    x_steps = sorted(range(1, side), key=lambda d: -min(d, side - d))
    z_steps = sorted(range(1, depth_z), key=lambda d: -min(d, depth_z - d))

    def x_at(step):
        return lax.rem(x + step, side)

    def z_at(step):
        return lax.rem(z + step, depth_z)

    barrier = pltpu.get_barrier_semaphore()
    peers = [partner, beside]
    peers += [at(x_at(d), y, core) for d in range(1, side)]
    peers += [at(x, lax.rem(y + d, side), c) for d in range(1, side) for c in range(CORES)]
    peers += [(me, z_at(d)) for d in range(1, depth_z)]
    for peer in peers:
        pl.semaphore_signal(barrier, inc=1, device_id=peer, device_id_type=MESH)
    pl.semaphore_wait(barrier, len(peers))

    def remote(source, target, sent, got, device):
        return pltpu.make_async_remote_copy(
            src_ref=source, dst_ref=target, send_sem=sent, recv_sem=got, device_id=device, device_id_type=MESH
        )

    size = grads.shape[1]
    core_copies = []
    for d in x_steps + [0]:
        row = x_at(d)
        copy = remote(packed.at[1 - core, row], from_core.at[row], core_sent.at[row], core_got.at[row], partner)
        copy.start()
        core_copies.append(copy)
    move = remote(grads.at[1], grad_out.at[pl.ds(size, size)], move_sent, move_got, following)
    move.start()
    stay = pltpu.make_async_copy(grads.at[0], grad_out.at[pl.ds(0, size)], stay_done)
    stay.start()

    x_copies = []
    for d in x_steps:
        row = x_at(d)
        remote(packed.at[1 - core, row], from_core.at[row], core_sent.at[row], core_got.at[row], partner).wait_recv()
        sum_core[row] = packed[core, row] + from_core[row]
        copy = remote(sum_core.at[row], from_x.at[d - 1], x_sent.at[d - 1], x_got.at[d - 1], at(row, y, core))
        copy.start()
        x_copies.append(copy)
    remote(packed.at[1 - core, x], from_core.at[x], core_sent.at[x], core_got.at[x], partner).wait_recv()
    total = packed[core, x] + from_core[x]
    for d in reversed(x_steps):
        remote(sum_core.at[x], from_x.at[d - 1], x_sent.at[d - 1], x_got.at[d - 1], at(x, y, core)).wait_recv()
        total = total + from_x[d - 1]
    sum_x[...] = total

    holder = lax.div(y, share)
    y_copies = []
    for j in range(share):
        for c in range(CORES):
            goal = share * core + j
            away = jnp.logical_or(goal != y, core != c)
            copy = remote(
                sum_x.at[j], from_y.at[y], y_sent.at[j * CORES + c], y_got.at[y], at(x, goal, c)
            )
            pl.when(away)(copy.start)
            y_copies.append((away, copy))

    @pl.when(holder == core)
    def _():
        from_y[y] = sum_x[lax.rem(y, share)]

    for s in range(side):
        arrives = jnp.logical_or(s != y, holder != core)
        waiter = remote(sum_x.at[0], from_y.at[s], y_sent.at[0], y_got.at[s], at(x, s, holder))
        pl.when(arrives)(waiter.wait_recv)
    total = from_y[0]
    for s in range(1, side):
        total = total + from_y[s]
    sum_y[...] = total
    z_copies = []
    for d in z_steps:
        copy = remote(sum_y, from_z.at[z], z_sent.at[d - 1], z_got.at[z], (me, z_at(d)))
        copy.start()
        z_copies.append(copy)
    from_z[z] = total
    for d in z_steps:
        source = z_at(d)
        remote(sum_y, from_z.at[source], z_sent.at[d - 1], z_got.at[source], (me, source)).wait_recv()
    total = from_z[0]
    for s in range(1, depth_z):
        total = total + from_z[s]
    total = total * (1.0 / divisor)

    pieces = [total] + [pltpu.roll(total, LANES - KEEP * a, 1) for a in range(1, LANES // KEEP)]
    held = TILE * len(pieces)
    square = jnp.concatenate(pieces + [jnp.zeros((LANES - held, LANES), jnp.float32)], axis=0).T
    own = held // CORES
    square = jnp.where(core == 1, pltpu.roll(square, LANES - own, 1), square)
    taps = kernel_out.shape[0]
    kernel_out[...] = square[:taps, :own]
    norm_out[...] = square[taps : taps + 2, :own]

    for copy in core_copies + x_copies + z_copies:
        copy.wait_send()
    for away, copy in y_copies:
        pl.when(away)(copy.wait_send)
    stay.wait()
    move.wait()


def share_pass(grads, packed, taps):
    side = packed.shape[1]
    depth_z = lax.axis_size("group")
    share = side // CORES
    size, channels = grads.shape[1:]
    frames = CORES * size
    divisor = math.sqrt(lax.axis_size("dp") * depth_z * frames)
    own = channels // lax.axis_size("dp")
    vmem = pl.BlockSpec(memory_space=pltpu.VMEM)
    f32 = jnp.float32
    dma = pltpu.SemaphoreType.DMA
    return pl.pallas_call(
        lambda *refs: share_kernel(side, depth_z, divisor, *refs),
        out_shape=(
            jax.ShapeDtypeStruct((frames, channels), jnp.bfloat16),
            jax.ShapeDtypeStruct((taps, own), f32),
            jax.ShapeDtypeStruct((2, own), f32),
        ),
        in_specs=[vmem, vmem],
        out_specs=[pl.BlockSpec(memory_space=pl.ANY), vmem, vmem],
        scratch_shapes=[
            pltpu.VMEM((side, share, TILE, LANES), f32),
            pltpu.VMEM((side, share, TILE, LANES), f32),
            pltpu.VMEM((side - 1, share, TILE, LANES), f32),
            pltpu.VMEM((share, TILE, LANES), f32),
            pltpu.VMEM((side, TILE, LANES), f32),
            pltpu.VMEM((TILE, LANES), f32),
            pltpu.VMEM((depth_z, TILE, LANES), f32),
            dma((side,)), dma((side,)),
            dma((side - 1,)), dma((side - 1,)),
            dma((side,)), dma((side,)),
            dma((depth_z - 1,)), dma((depth_z,)),
            dma, dma, dma,
        ],
        compiler_params=pltpu.CompilerParams(collective_id=0, has_side_effects=True),
        name="share_terms",
    )(grads, packed)


def local(features, cotangent, lengths, destination, kernel, norm_gain, norm_bias):
    frames, channels = features.shape[2:]
    side = math.isqrt(lax.axis_size("dp") // CORES)
    grads, packed = local_pass(
        features[0, 0], cotangent[0, 0], lengths[0, 0], destination[0, 0], kernel, norm_gain, norm_bias, side
    )
    input_grad, kernel_grad, norm_grad = share_pass(grads, packed, kernel.shape[0])
    return (input_grad.reshape(1, 1, frames, channels), kernel_grad, norm_grad)


def solution(mesh):
    return jax.shard_map(
        local,
        mesh=mesh,
        in_specs=(
            P("dp", "group", None, None),
            P("dp", "group", None, None),
            P("dp", "group", None),
            P("dp", "group", None),
            P(),
            P(),
            P(),
        ),
        out_specs=(P("dp", "group", None, None), P(None, "dp"), P(None, "dp")),
        check_vma=False,
    )
```

time: 609 us -> 70.5 us (0.12); the launches traced: 598 us -> 70.2 us
  blocking collectives: 525 us -> 0 us
  Pallas kernels: 0 us -> 63.6 us
  other arithmetic: 42.4 us -> 0 us
  between operations: 15.2 us -> 0.65 us
    unnamed x1 -> x0, blocking collectives: 502 us -> none
    pallas_call x0 -> x2, Pallas kernels: none -> 63.6 us  [the longest x1 39.9 us: share_pass(): pl.pallas_call(lambda *refs: share_kernel(side, depth_z, divisor, *refs),...]
    reduce_sum x8 -> x0, other arithmetic: 26.7 us -> none  [the longest x4 12.5 us: param_terms(): jnp.sum(weighted * padded[tap_index:tap_index + frames], axis=0)]
    psum x1 -> x0, blocking collectives: 23.3 us -> none  [local(): whole_sums = lax.psum((kernel_term, norm_term), 'group')]
    convert_element_type x3 -> x0, other arithmetic: 10.9 us -> none  [the longest x1 9.51 us: grad_rows(): return total.astype(jnp.bfloat16)]
  transfers between devices with their start and end apart: 2 -> 0, of which waited for: 0 -> 0; matrix products, arithmetic and copies ran while one was open for 3% -> 0% of each run, Pallas kernels for 0% -> 0%
where the time goes in v1:
time: 70.5 us; the launch traced here: 70.2 us
  Pallas kernels  63.6 us (90%)
  local copies, waits for them, and re-layouts  5.92 us (8%)
    pallas_call x1, Pallas kernels, share_pass(): pl.pallas_call(lambda *refs: share_kernel(side, depth_z, divisor, *refs),...  39.9 us
    pallas_call x1, Pallas kernels, local_pass(): pl.pallas_call(local_kernel, out_shape=(jax.ShapeDtypeStruct((2, size, ch...  23.7 us
    unnamed x7, local copies, waits for them, and re-layouts  4.03 us

profile of v1, /device:TPU:1, one launch (start us, length us, event | category | flops | bytes accessed | tf_op | source)
XLA Modules:
  0.0 70.2 jit_solution(12267831876060193529)
XLA Ops:
  0.6 0.0 copy-start
  0.6 1.3 %broadcast_in_dim.6.gain = f32[1,1536]{1,0:T(1,128)} reshape(f32[1536]{0:T(1024)} %param.12) | data formatting | bytes 12288 | tf_op jit(solution)/shard_map/broadcast_in_dim | solution.py:209
  1.9 0.0 copy-done
  1.9 0.6 broadcast_in_dim.7.bias
  2.5 23.7 %conv_block.1 = (bf16[2,128,1536]{2,1,0:T(8,128)(2,1)}, f32[2,8,4,8,128]{4,3,2,1,0:T(8,128)}) custom-call(s32[4]{0:T(128)} %bitcast.8, s32[2]{0:T(128)} %bitcast.9, bf16[256,1536]{1,0:T(8,128)(2,1)} %bitcast.5, bf16[256,1536]{1,0:T(8,128)(2,1)} %bitcast.6, f32[31,1536]{1,0:T(8,128)} %kernel.1, f32[1,1536]{1,0:T(1,128)} %broadcast_in_dim.6.gain, ...), custom_call_target="tpu_custom_call" | custom-call | tf_op jit(solution)/shard_map/conv_block/pallas_call | solution.py:185
  26.3 39.9 %share_terms.1 = (bf16[256,1536]{1,0:T(8,128)(2,1)}, f32[31,12]{1,0:T(8,128)}, f32[2,12]{1,0:T(2,128)}) custom-call(bf16[2,128,1536]{2,1,0:T(8,128)(2,1)} %get-tuple-element.8.refs_0_, f32[2,8,4,8,128]{4,3,2,1,0:T(8,128)} %get-tuple-element.9.refs_1_), custom_call_target="tpu_custom_call" | custom-call | tf_op jit(solution)/shard_map/share_terms/pallas_call | solution.py:350
  66.2 1.4 %copy.10 = f32[31,12]{0,1:T(8,128)} copy(f32[31,12]{1,0:T(8,128)} %get-tuple-element.14) | data formatting | bytes 2976
  67.6 0.0 copy-start.1
  67.6 2.1 %copy.13 = bf16[1,1,256,1536]{3,2,1,0:T(8,128)(2,1)} copy(bf16[1,1,256,1536]{3,2,1,0:T(8,128)(2,1)} %bitcast.7) | data formatting | bytes 1572864
  69.6 0.0 copy-done.1
  69.6 0.6 copy.14
Async XLA Ops:
  0.6 1.3 %copy-start = (f32[1536]{0:T(1024)S(1)}, f32[1536]{0:T(1024)}, u32[]{:S(2)}) copy-start(f32[1536]{0:T(1024)} %param.13) | copy-start | bytes 18436
  67.6 2.1 %copy-start.1 = (f32[2,12]{1,0:T(2,128)S(1)}, f32[2,12]{1,0:T(2,128)}, u32[]{:S(2)}) copy-start(f32[2,12]{1,0:T(2,128)} %get-tuple-element.21) | copy-start | bytes 292

commit v2 on v1

--- a/solution.py
+++ b/solution.py
@@ -13,6 +13,7 @@
 KEEP = 40
 TILE = 8
 CORES = 2
+MOVES = 3
 MESH = pl.DeviceIdType.MESH
 
 
@@ -30,11 +31,46 @@
     return total
 
 
-def local_kernel(
+def block_kernel(
+    side, depth_z, divisor,
     lengths, destination, features, cotangent, kernel, gain, bias,
-    grad_out, packed_out,
-    stage, padded, conv, dnorm, dconv, owner, row_a, row_b, mean, scale, tap_sums, terms, columnwise,
+    grad_out, tile_out,
+    stage, padded, conv, dnorm, dconv, owner, row_a, row_b, mean, scale, tap_sums, terms, columnwise, packed, grads,
+    from_core, sum_core, from_x, sum_x, from_y, sum_y, from_z,
+    core_sent, core_got, x_sent, x_got, y_sent, y_got, z_sent, z_got, move_sent, move_got, stay_done,
 ):
+    me = lax.axis_index("dp")
+    z = lax.axis_index("group")
+    ring = side * side * CORES
+    core = lax.rem(me, CORES)
+    chip = lax.div(me, CORES)
+    y = lax.rem(chip, side)
+    x = lax.div(chip, side)
+    share = side // CORES
+
+    def at(x, y, core):
+        return ((x * side + y) * CORES + core, z)
+
+    partner = at(x, y, 1 - core)
+    following = (lax.rem(me + 1, ring), z)
+    beside = (lax.rem(me + ring + 2 * core - 1, ring), z)
+    x_steps = sorted(range(1, side), key=lambda d: -min(d, side - d))
+    z_steps = sorted(range(1, depth_z), key=lambda d: -min(d, depth_z - d))
+
+    def x_at(step):
+        return lax.rem(x + step, side)
+
+    def z_at(step):
+        return lax.rem(z + step, depth_z)
+
+    barrier = pltpu.get_barrier_semaphore()
+    peers = [partner, beside]
+    peers += [at(x_at(d), y, core) for d in range(1, side)]
+    peers += [at(x, lax.rem(y + d, side), c) for d in range(1, side) for c in range(CORES)]
+    peers += [(me, z_at(d)) for d in range(1, depth_z)]
+    for peer in peers:
+        pl.semaphore_signal(barrier, inc=1, device_id=peer, device_id_type=MESH)
+
     frames, channels = features.shape
     utterances = lengths.shape[0]
     taps = kernel.shape[0]
@@ -105,8 +141,8 @@
     def _(b):
         normed = conv[b] * scale[...]
         conv[b] = normed
-        g = gain[:, columns(b)]
-        act = normed * g + bias[:, columns(b)]
+        g = gain[columns(b)][None]
+        act = normed * g + bias[columns(b)][None]
         gate = jax.nn.sigmoid(act)
         dact = spread_rows(cotangent[:, columns(b)].astype(jnp.float32)) * gate * (1.0 + act * (1.0 - gate))
         terms[pl.ds(taps, 1), columns(b)] = jnp.sum(dact * normed, axis=0, keepdims=True)
@@ -138,7 +174,7 @@
         square = jnp.concatenate([terms[:, columns(b)], jnp.zeros((LANES - KEEP, LANES), jnp.float32)], axis=0)
         columnwise[columns(b), :] = square.T
 
-    halves, lines, share = packed_out.shape[:3]
+    halves, lines, share = packed.shape[:3]
     depth = channels // (halves * lines * share)
 
     @pl.loop(0, lines)
@@ -150,10 +186,11 @@
                 piece = columnwise[pl.ds(pl.multiple_of(first + TILE * a, TILE), TILE), :]
                 piece = piece if a == 0 else pltpu.roll(piece, KEEP * a, 1)
                 tile = piece if tile is None else tile + piece
-            packed_out[y // share, x, y % share] = tile
-
-    @pl.loop(0, blocks)
-    def _(b):
+            packed[y // share, x, y % share] = tile
+
+    size = frames // destination.shape[0]
+
+    def input_gradient(b):
         for c in range(2):
             stage[pl.ds(chunk * c, chunk), :] = convolve(
                 dconv.at[b], GAP - half_span + chunk * c,
@@ -165,107 +202,36 @@
         for u in range(1, utterances):
             grad = jnp.where(spot >= begin, stage[pl.ds(GAP * u, frames), :], grad)
             begin = begin + lengths[u]
-        grad = grad.astype(grad_out.dtype)
-        size = grad_out.shape[1]
-        for i in range(frames // size):
-            grad_out[destination[i], :, columns(b)] = grad[size * i : size * (i + 1)]
-
-
-def local_pass(features, cotangent, lengths, destination, kernel, gain, bias, side=8):
-    frames, channels = features.shape
-    utterances = lengths.shape[0]
-    taps = kernel.shape[0]
-    size = frames // destination.shape[0]
-    blocks = channels // LANES
-    spread = frames + GAP * (utterances - 1)
-    margin = GAP * (utterances - 1)
-    smem = pl.BlockSpec(memory_space=pltpu.SMEM)
-    vmem = pl.BlockSpec(memory_space=pltpu.VMEM)
-    f32 = jnp.float32
-    return pl.pallas_call(
-        local_kernel,
-        out_shape=(
-            jax.ShapeDtypeStruct((2, size, channels), jnp.bfloat16),
-            jax.ShapeDtypeStruct((CORES, side, side // CORES, TILE, LANES), f32),
-        ),
-        in_specs=[smem, smem] + [vmem] * 5,
-        out_specs=[vmem, vmem],
-        scratch_shapes=[
-            pltpu.VMEM((margin + spread, LANES), f32),
-            pltpu.VMEM((blocks, spread + 2 * GAP, LANES), f32),
-            pltpu.VMEM((blocks, spread, LANES), f32),
-            pltpu.VMEM((blocks, spread, LANES), f32),
-            pltpu.VMEM((blocks, spread + 2 * GAP, LANES), f32),
-            pltpu.VMEM((spread, LANES), jnp.int32),
-            pltpu.VMEM((spread, LANES), f32),
-            pltpu.VMEM((spread, LANES), f32),
-            pltpu.VMEM((spread, LANES), f32),
-            pltpu.VMEM((spread, LANES), f32),
-            pltpu.VMEM((taps, TILE, LANES), f32),
-            pltpu.VMEM((KEEP, channels), f32),
-            pltpu.VMEM((channels, LANES), f32),
-        ],
-        name="conv_block",
-    )(lengths, destination, features, cotangent, kernel, gain[None], bias[None])
-
-
-def share_kernel(
-    side, depth_z, divisor,
-    grads, packed,
-    grad_out, kernel_out, norm_out,
-    from_core, sum_core, from_x, sum_x, from_y, sum_y, from_z,
-    core_sent, core_got, x_sent, x_got, y_sent, y_got, z_sent, z_got, move_sent, move_got, stay_done,
-):
-    me = lax.axis_index("dp")
-    z = lax.axis_index("group")
-    ring = side * side * CORES
-    core = lax.rem(me, CORES)
-    chip = lax.div(me, CORES)
-    y = lax.rem(chip, side)
-    x = lax.div(chip, side)
-    share = side // CORES
-
-    def at(x, y, core):
-        return ((x * side + y) * CORES + core, z)
-
-    partner = at(x, y, 1 - core)
-    following = (lax.rem(me + 1, ring), z)
-    beside = (lax.rem(me + ring + 2 * core - 1, ring), z)
-    x_steps = sorted(range(1, side), key=lambda d: -min(d, side - d))
-    z_steps = sorted(range(1, depth_z), key=lambda d: -min(d, depth_z - d))
-
-    def x_at(step):
-        return lax.rem(x + step, side)
-
-    def z_at(step):
-        return lax.rem(z + step, depth_z)
-
-    barrier = pltpu.get_barrier_semaphore()
-    peers = [partner, beside]
-    peers += [at(x_at(d), y, core) for d in range(1, side)]
-    peers += [at(x, lax.rem(y + d, side), c) for d in range(1, side) for c in range(CORES)]
-    peers += [(me, z_at(d)) for d in range(1, depth_z)]
-    for peer in peers:
-        pl.semaphore_signal(barrier, inc=1, device_id=peer, device_id_type=MESH)
-    pl.semaphore_wait(barrier, len(peers))
+        top, bottom = grad[:size], grad[size:]
+        keep_top = destination[0] == 0
+        grads[0, :, columns(b)] = jnp.where(keep_top, top, bottom).astype(grads.dtype)
+        grads[1, :, columns(b)] = jnp.where(keep_top, bottom, top).astype(grads.dtype)
 
     def remote(source, target, sent, got, device):
         return pltpu.make_async_remote_copy(
             src_ref=source, dst_ref=target, send_sem=sent, recv_sem=got, device_id=device, device_id_type=MESH
         )
 
-    size = grads.shape[1]
+    batch = blocks // MOVES
+    moves = []
+
+    def gradient_batch(i):
+        pl.loop(batch * i, batch * (i + 1))(input_gradient)
+        part = pl.ds(batch * LANES * i, batch * LANES)
+        move = remote(
+            grads.at[1, :, part], grad_out.at[pl.ds(size, size), part], move_sent.at[i], move_got.at[i], following
+        )
+        move.start()
+        moves.append(move)
+
+    pl.semaphore_wait(barrier, len(peers))
     core_copies = []
     for d in x_steps + [0]:
         row = x_at(d)
         copy = remote(packed.at[1 - core, row], from_core.at[row], core_sent.at[row], core_got.at[row], partner)
         copy.start()
         core_copies.append(copy)
-    move = remote(grads.at[1], grad_out.at[pl.ds(size, size)], move_sent, move_got, following)
-    move.start()
-    stay = pltpu.make_async_copy(grads.at[0], grad_out.at[pl.ds(0, size)], stay_done)
-    stay.start()
-
+    gradient_batch(0)
     x_copies = []
     for d in x_steps:
         row = x_at(d)
@@ -274,6 +240,11 @@
         copy = remote(sum_core.at[row], from_x.at[d - 1], x_sent.at[d - 1], x_got.at[d - 1], at(row, y, core))
         copy.start()
         x_copies.append(copy)
+    for i in range(1, MOVES):
+        gradient_batch(i)
+    stay = pltpu.make_async_copy(grads.at[0], grad_out.at[pl.ds(0, size)], stay_done)
+    stay.start()
+
     remote(packed.at[1 - core, x], from_core.at[x], core_sent.at[x], core_got.at[x], partner).wait_recv()
     total = packed[core, x] + from_core[x]
     for d in reversed(x_steps):
@@ -317,46 +288,57 @@
     total = from_z[0]
     for s in range(1, depth_z):
         total = total + from_z[s]
-    total = total * (1.0 / divisor)
-
-    pieces = [total] + [pltpu.roll(total, LANES - KEEP * a, 1) for a in range(1, LANES // KEEP)]
-    held = TILE * len(pieces)
-    square = jnp.concatenate(pieces + [jnp.zeros((LANES - held, LANES), jnp.float32)], axis=0).T
-    own = held // CORES
-    square = jnp.where(core == 1, pltpu.roll(square, LANES - own, 1), square)
-    taps = kernel_out.shape[0]
-    kernel_out[...] = square[:taps, :own]
-    norm_out[...] = square[taps : taps + 2, :own]
+    tile_out[...] = total * (1.0 / divisor)
 
     for copy in core_copies + x_copies + z_copies:
         copy.wait_send()
     for away, copy in y_copies:
         pl.when(away)(copy.wait_send)
     stay.wait()
-    move.wait()
-
-
-def share_pass(grads, packed, taps):
-    side = packed.shape[1]
+    for move in moves:
+        move.wait()
+
+
+def block_pass(features, cotangent, lengths, destination, kernel, gain, bias):
+    frames, channels = features.shape
+    utterances = lengths.shape[0]
+    taps = kernel.shape[0]
+    size = frames // destination.shape[0]
+    blocks = channels // LANES
+    spread = frames + GAP * (utterances - 1)
+    margin = GAP * (utterances - 1)
+    side = math.isqrt(lax.axis_size("dp") // CORES)
+    share = side // CORES
     depth_z = lax.axis_size("group")
-    share = side // CORES
-    size, channels = grads.shape[1:]
-    frames = CORES * size
     divisor = math.sqrt(lax.axis_size("dp") * depth_z * frames)
-    own = channels // lax.axis_size("dp")
+    smem = pl.BlockSpec(memory_space=pltpu.SMEM)
     vmem = pl.BlockSpec(memory_space=pltpu.VMEM)
     f32 = jnp.float32
     dma = pltpu.SemaphoreType.DMA
     return pl.pallas_call(
-        lambda *refs: share_kernel(side, depth_z, divisor, *refs),
+        lambda *refs: block_kernel(side, depth_z, divisor, *refs),
         out_shape=(
             jax.ShapeDtypeStruct((frames, channels), jnp.bfloat16),
-            jax.ShapeDtypeStruct((taps, own), f32),
-            jax.ShapeDtypeStruct((2, own), f32),
+            jax.ShapeDtypeStruct((TILE, LANES), f32),
         ),
-        in_specs=[vmem, vmem],
-        out_specs=[pl.BlockSpec(memory_space=pl.ANY), vmem, vmem],
+        in_specs=[smem, smem] + [vmem] * 5,
+        out_specs=[pl.BlockSpec(memory_space=pl.ANY), vmem],
         scratch_shapes=[
+            pltpu.VMEM((margin + spread, LANES), f32),
+            pltpu.VMEM((blocks, spread + 2 * GAP, LANES), f32),
+            pltpu.VMEM((blocks, spread, LANES), f32),
+            pltpu.VMEM((blocks, spread, LANES), f32),
+            pltpu.VMEM((blocks, spread + 2 * GAP, LANES), f32),
+            pltpu.VMEM((spread, LANES), jnp.int32),
+            pltpu.VMEM((spread, LANES), f32),
+            pltpu.VMEM((spread, LANES), f32),
+            pltpu.VMEM((spread, LANES), f32),
+            pltpu.VMEM((spread, LANES), f32),
+            pltpu.VMEM((taps, TILE, LANES), f32),
+            pltpu.VMEM((KEEP, channels), f32),
+            pltpu.VMEM((channels, LANES), f32),
+            pltpu.VMEM((CORES, side, share, TILE, LANES), f32),
+            pltpu.VMEM((2, size, channels), jnp.bfloat16),
             pltpu.VMEM((side, share, TILE, LANES), f32),
             pltpu.VMEM((side, share, TILE, LANES), f32),
             pltpu.VMEM((side - 1, share, TILE, LANES), f32),
@@ -368,21 +350,50 @@
             dma((side - 1,)), dma((side - 1,)),
             dma((side,)), dma((side,)),
             dma((depth_z - 1,)), dma((depth_z,)),
-            dma, dma, dma,
+            dma((MOVES,)), dma((MOVES,)), dma,
         ],
         compiler_params=pltpu.CompilerParams(collective_id=0, has_side_effects=True),
-        name="share_terms",
-    )(grads, packed)
+        name="conv_block",
+    )(lengths, destination, features, cotangent, kernel, gain, bias)
+
+
+def finish_kernel(grads, tile, grad_out, kernel_out, norm_out, done):
+    copy = pltpu.make_async_copy(grads, grad_out, done)
+    copy.start()
+    core = lax.rem(lax.axis_index("dp"), CORES)
+    total = tile[...]
+    pieces = [total] + [pltpu.roll(total, LANES - KEEP * a, 1) for a in range(1, LANES // KEEP)]
+    square = jnp.concatenate(pieces, axis=0)
+    own, taps = kernel_out.shape
+    square = jnp.where(core == 1, square[own:], square[:own])
+    kernel_out[...] = square[:, :taps]
+    norm_out[...] = square[:, taps : taps + 2].T
+    copy.wait()
+
+
+def finish_pass(grads, tile, taps):
+    own = grads.shape[1] // lax.axis_size("dp")
+    vmem = pl.BlockSpec(memory_space=pltpu.VMEM)
+    return pl.pallas_call(
+        finish_kernel,
+        out_shape=(
+            jax.ShapeDtypeStruct(grads.shape, grads.dtype),
+            jax.ShapeDtypeStruct((own, taps), jnp.float32),
+            jax.ShapeDtypeStruct((2, own), jnp.float32),
+        ),
+        in_specs=[vmem, vmem],
+        out_specs=[pl.BlockSpec(memory_space=pl.ANY), vmem, vmem],
+        scratch_shapes=[pltpu.SemaphoreType.DMA],
+        name="finish",
+    )(grads, tile)
 
 
 def local(features, cotangent, lengths, destination, kernel, norm_gain, norm_bias):
-    frames, channels = features.shape[2:]
-    side = math.isqrt(lax.axis_size("dp") // CORES)
-    grads, packed = local_pass(
-        features[0, 0], cotangent[0, 0], lengths[0, 0], destination[0, 0], kernel, norm_gain, norm_bias, side
+    grads, tile = block_pass(
+        features[0, 0], cotangent[0, 0], lengths[0, 0], destination[0, 0], kernel, norm_gain, norm_bias
     )
-    input_grad, kernel_grad, norm_grad = share_pass(grads, packed, kernel.shape[0])
-    return (input_grad.reshape(1, 1, frames, channels), kernel_grad, norm_grad)
+    input_grad, kernel_grad, norm_grad = finish_pass(grads, tile, kernel.shape[0])
+    return (input_grad.reshape(features.shape), kernel_grad.T, norm_grad)
 
 
 def solution(mesh):

time: 70.5 us -> 58.3 us (0.83)
  Pallas kernels: 63.6 us -> 57.4 us
  local copies, waits for them, and re-layouts: 5.92 us -> 0 us
    pallas_call x2, Pallas kernels: 63.6 us -> 57.4 us  [the longest x1 54.8 us: block_pass(): pl.pallas_call(lambda *refs: block_kernel(side, depth_z, divisor, *refs),...]
    unnamed x7 -> x0, local copies, waits for them, and re-layouts: 4.03 us -> none
    broadcast_in_dim x2 -> x0, local copies, waits for them, and re-layouts: 1.89 us -> none  [the longest x1 1.3 us: local_pass(): gain[None]]
where the time goes in v2:
time: 58.3 us; the launch traced here: 58.1 us
  Pallas kernels  57.4 us (98%)
  between operations  0.64 us (1%)
    pallas_call x1, Pallas kernels, block_pass(): pl.pallas_call(lambda *refs: block_kernel(side, depth_z, divisor, *refs),...  54.8 us
    pallas_call x1, Pallas kernels, finish_pass(): pl.pallas_call(finish_kernel, out_shape=(jax.ShapeDtypeStruct(grads.shape...  2.62 us

profile of v2, /device:TPU:1, one launch (start us, length us, event | category | flops | bytes accessed | tf_op | source)
XLA Modules:
  0.0 58.1 jit_solution(921374230254349086)
XLA Ops:
  0.6 54.8 %conv_block.1 = (bf16[256,1536]{1,0:T(8,128)(2,1)}, f32[8,128]{1,0:T(8,128)}) custom-call(s32[4]{0:T(128)} %bitcast.8, s32[2]{0:T(128)} %bitcast.9, bf16[256,1536]{1,0:T(8,128)(2,1)} %bitcast.6, bf16[256,1536]{1,0:T(8,128)(2,1)} %bitcast.7, f32[31,1536]{1,0:T(8,128)} %refs_4_.1, f32[1536]{0:T(1024)} %refs_5_.1, f32[1536]{0:T(1024)} %refs_6_.1), custom_call_target="tpu_custom_call" | custom-call | tf_op jit(solution)/shard_map/conv_block/pallas_call | solution.py:318
  55.4 2.6 %finish.1 = (bf16[256,1536]{1,0:T(8,128)(2,1)}, f32[12,31]{1,0:T(8,128)}, f32[2,12]{1,0:T(2,128)}) custom-call(bf16[256,1536]{1,0:T(8,128)(2,1)} %get-tuple-element.8.grads, f32[8,128]{1,0:T(8,128)} %get-tuple-element.9.tile), custom_call_target="tpu_custom_call" | custom-call | tf_op jit(solution)/shard_map/finish/pallas_call | solution.py:377

commit v3 on v2

--- a/solution.py
+++ b/solution.py
@@ -13,7 +13,8 @@
 KEEP = 40
 TILE = 8
 CORES = 2
-MOVES = 3
+MOVES = 4
+PAIR = 2
 MESH = pl.DeviceIdType.MESH
 
 
@@ -89,18 +90,22 @@
         here = (place >= begin + GAP * u) & (place < finish + GAP * u)
         wide_owner = jnp.where(here, u, wide_owner)
         begin = finish
-    owner[...] = wide_owner
+    owner[...] = wide_owner.astype(jnp.float32).astype(jnp.bfloat16)
 
     edge = jnp.zeros((GAP, LANES), jnp.float32)
     terms[...] = jnp.zeros_like(terms)
 
     def spread_rows(value):
-        stage[pl.ds(margin, frames), :] = value
         ids = owner[...]
-        out = jnp.zeros((spread, LANES), jnp.float32)
+        out = jnp.zeros((spread, LANES), value.dtype)
         for u in range(utterances):
-            out = jnp.where(ids == u, stage[pl.ds(margin - GAP * u, spread), :], out)
-        return out
+            parts = [value]
+            if u > 0:
+                parts = [jnp.zeros((GAP * u, LANES), value.dtype)] + parts
+            if u < utterances - 1:
+                parts = parts + [jnp.zeros((margin - GAP * u, LANES), value.dtype)]
+            out = jnp.where(ids == u, jnp.concatenate(parts, axis=0), out)
+        return out.astype(jnp.float32)
 
     def columns(b):
         return pl.ds(pl.multiple_of(b * LANES, LANES), LANES)
@@ -108,14 +113,13 @@
     def row_total(ref):
         return jnp.broadcast_to(jnp.sum(ref[...], axis=1, keepdims=True), (spread, LANES))
 
-    stage[...] = jnp.zeros_like(stage)
     row_a[...] = jnp.zeros_like(row_a)
 
     @pl.loop(0, blocks)
     def _(b):
         padded[b, pl.ds(0, GAP), :] = edge
         padded[b, pl.ds(GAP + spread, GAP), :] = edge
-        padded[b, pl.ds(GAP, spread), :] = spread_rows(features[:, columns(b)].astype(jnp.float32))
+        padded[b, pl.ds(GAP, spread), :] = spread_rows(features[:, columns(b)])
         for c in range(2):
             value = convolve(
                 padded.at[b], GAP - half_span + chunk * c,
@@ -143,8 +147,8 @@
         conv[b] = normed
         g = gain[columns(b)][None]
         act = normed * g + bias[columns(b)][None]
-        gate = jax.nn.sigmoid(act)
-        dact = spread_rows(cotangent[:, columns(b)].astype(jnp.float32)) * gate * (1.0 + act * (1.0 - gate))
+        gate = 0.5 * jnp.tanh(0.5 * act) + 0.5
+        dact = spread_rows(cotangent[:, columns(b)]) * gate * (1.0 + act * (1.0 - gate))
         terms[pl.ds(taps, 1), columns(b)] = jnp.sum(dact * normed, axis=0, keepdims=True)
         terms[pl.ds(taps + 1, 1), columns(b)] = jnp.sum(dact, axis=0, keepdims=True)
         weighted = dact * g
@@ -155,8 +159,7 @@
     mean[...] = row_total(row_a) * inverse
     row_b[...] = row_total(row_b) * inverse
 
-    @pl.loop(0, blocks)
-    def _(b):
+    def kernel_terms(b):
         dconv[b, pl.ds(0, GAP), :] = edge
         dconv[b, pl.ds(GAP + spread, GAP), :] = edge
         dconv[b, pl.ds(GAP, spread), :] = scale[...] * (dnorm[b] - mean[...] - conv[b] * row_b[...])
@@ -174,19 +177,50 @@
         square = jnp.concatenate([terms[:, columns(b)], jnp.zeros((LANES - KEEP, LANES), jnp.float32)], axis=0)
         columnwise[columns(b), :] = square.T
 
-    halves, lines, share = packed.shape[:3]
-    depth = channels // (halves * lines * share)
-
-    @pl.loop(0, lines)
-    def _(x):
-        for y in range(halves * share):
-            first = (x * halves * share + y) * depth
+    depth = channels // (side * side)
+
+    def pack_row(row):
+        for column in range(side):
+            first = (row * side + column) * depth
             tile = None
             for a in range(depth // TILE):
                 piece = columnwise[pl.ds(pl.multiple_of(first + TILE * a, TILE), TILE), :]
                 piece = piece if a == 0 else pltpu.roll(piece, KEEP * a, 1)
                 tile = piece if tile is None else tile + piece
-            packed[y // share, x, y % share] = tile
+            packed[column // share, row, column % share] = tile
+
+    def remote(source, target, sent, got, device):
+        return pltpu.make_async_remote_copy(
+            src_ref=source, dst_ref=target, send_sem=sent, recv_sem=got, device_id=device, device_id_type=MESH
+        )
+
+    def core_copy(row):
+        return remote(packed.at[1 - core, row], from_core.at[row], core_sent.at[row], core_got.at[row], partner)
+
+    def x_copy(row, d):
+        return remote(sum_core.at[row], from_x.at[d], x_sent.at[d], x_got.at[d], at(row, y, core))
+
+    def forward(pair):
+        for r in range(PAIR):
+            row = pair * PAIR + r
+            core_copy(row).wait_recv()
+            sum_core[row] = packed[core, row] + from_core[row]
+            d = lax.rem(row - x + side, side)
+            pl.when(d != 0)(x_copy(row, d).start)
+
+    pl.semaphore_wait(barrier, len(peers))
+    groups = side // PAIR
+    width = blocks // groups
+    own_pair = lax.div(x, PAIR)
+
+    @pl.loop(0, groups)
+    def _(i):
+        pair = lax.rem(own_pair + 1 + i, groups)
+        pl.loop(0, width)(lambda t: kernel_terms(pair * width + t))
+        for r in range(PAIR):
+            pack_row(pair * PAIR + r)
+            core_copy(pair * PAIR + r).start()
+        pl.when(i > 0)(lambda: forward(lax.rem(pair + groups - 1, groups)))
 
     size = frames // destination.shape[0]
 
@@ -207,11 +241,6 @@
         grads[0, :, columns(b)] = jnp.where(keep_top, top, bottom).astype(grads.dtype)
         grads[1, :, columns(b)] = jnp.where(keep_top, bottom, top).astype(grads.dtype)
 
-    def remote(source, target, sent, got, device):
-        return pltpu.make_async_remote_copy(
-            src_ref=source, dst_ref=target, send_sem=sent, recv_sem=got, device_id=device, device_id_type=MESH
-        )
-
     batch = blocks // MOVES
     moves = []
 
@@ -224,32 +253,13 @@
         move.start()
         moves.append(move)
 
-    pl.semaphore_wait(barrier, len(peers))
-    core_copies = []
-    for d in x_steps + [0]:
-        row = x_at(d)
-        copy = remote(packed.at[1 - core, row], from_core.at[row], core_sent.at[row], core_got.at[row], partner)
-        copy.start()
-        core_copies.append(copy)
     gradient_batch(0)
-    x_copies = []
-    for d in x_steps:
-        row = x_at(d)
-        remote(packed.at[1 - core, row], from_core.at[row], core_sent.at[row], core_got.at[row], partner).wait_recv()
-        sum_core[row] = packed[core, row] + from_core[row]
-        copy = remote(sum_core.at[row], from_x.at[d - 1], x_sent.at[d - 1], x_got.at[d - 1], at(row, y, core))
-        copy.start()
-        x_copies.append(copy)
-    for i in range(1, MOVES):
-        gradient_batch(i)
-    stay = pltpu.make_async_copy(grads.at[0], grad_out.at[pl.ds(0, size)], stay_done)
-    stay.start()
-
-    remote(packed.at[1 - core, x], from_core.at[x], core_sent.at[x], core_got.at[x], partner).wait_recv()
-    total = packed[core, x] + from_core[x]
+    forward(own_pair)
+    gradient_batch(1)
+    total = sum_core[x]
     for d in reversed(x_steps):
-        remote(sum_core.at[x], from_x.at[d - 1], x_sent.at[d - 1], x_got.at[d - 1], at(x, y, core)).wait_recv()
-        total = total + from_x[d - 1]
+        x_copy(x, d).wait_recv()
+        total = total + from_x[d]
     sum_x[...] = total
 
     holder = lax.div(y, share)
@@ -267,6 +277,11 @@
     @pl.when(holder == core)
     def _():
         from_y[y] = sum_x[lax.rem(y, share)]
+
+    for i in range(2, MOVES):
+        gradient_batch(i)
+    stay = pltpu.make_async_copy(grads.at[0], grad_out.at[pl.ds(0, size)], stay_done)
+    stay.start()
 
     for s in range(side):
         arrives = jnp.logical_or(s != y, holder != core)
@@ -290,7 +305,11 @@
         total = total + from_z[s]
     tile_out[...] = total * (1.0 / divisor)
 
-    for copy in core_copies + x_copies + z_copies:
+    for row in range(side):
+        core_copy(row).wait_send()
+    for d in x_steps:
+        x_copy(x_at(d), d).wait_send()
+    for copy in z_copies:
         copy.wait_send()
     for away, copy in y_copies:
         pl.when(away)(copy.wait_send)
@@ -318,18 +337,18 @@
     return pl.pallas_call(
         lambda *refs: block_kernel(side, depth_z, divisor, *refs),
         out_shape=(
-            jax.ShapeDtypeStruct((frames, channels), jnp.bfloat16),
-            jax.ShapeDtypeStruct((TILE, LANES), f32),
+            pltpu.VMEM((frames, channels), jnp.bfloat16),
+            pltpu.VMEM((TILE, LANES), f32),
         ),
         in_specs=[smem, smem] + [vmem] * 5,
-        out_specs=[pl.BlockSpec(memory_space=pl.ANY), vmem],
+        out_specs=[vmem, vmem],
         scratch_shapes=[
             pltpu.VMEM((margin + spread, LANES), f32),
             pltpu.VMEM((blocks, spread + 2 * GAP, LANES), f32),
             pltpu.VMEM((blocks, spread, LANES), f32),
             pltpu.VMEM((blocks, spread, LANES), f32),
             pltpu.VMEM((blocks, spread + 2 * GAP, LANES), f32),
-            pltpu.VMEM((spread, LANES), jnp.int32),
+            pltpu.VMEM((spread, LANES), jnp.bfloat16),
             pltpu.VMEM((spread, LANES), f32),
             pltpu.VMEM((spread, LANES), f32),
             pltpu.VMEM((spread, LANES), f32),
@@ -341,13 +360,13 @@
             pltpu.VMEM((2, size, channels), jnp.bfloat16),
             pltpu.VMEM((side, share, TILE, LANES), f32),
             pltpu.VMEM((side, share, TILE, LANES), f32),
-            pltpu.VMEM((side - 1, share, TILE, LANES), f32),
+            pltpu.VMEM((side, share, TILE, LANES), f32),
             pltpu.VMEM((share, TILE, LANES), f32),
             pltpu.VMEM((side, TILE, LANES), f32),
             pltpu.VMEM((TILE, LANES), f32),
             pltpu.VMEM((depth_z, TILE, LANES), f32),
             dma((side,)), dma((side,)),
-            dma((side - 1,)), dma((side - 1,)),
+            dma((side,)), dma((side,)),
             dma((side,)), dma((side,)),
             dma((depth_z - 1,)), dma((depth_z,)),
             dma((MOVES,)), dma((MOVES,)), dma,
@@ -385,7 +404,7 @@
         out_specs=[pl.BlockSpec(memory_space=pl.ANY), vmem, vmem],
         scratch_shapes=[pltpu.SemaphoreType.DMA],
         name="finish",
-    )(grads, tile)
+    )(pltpu.with_memory_space_constraint(grads, pltpu.VMEM), pltpu.with_memory_space_constraint(tile, pltpu.VMEM))
 
 
 def local(features, cotangent, lengths, destination, kernel, norm_gain, norm_bias):

time: 58.3 us -> 51.7 us (0.89)
  Pallas kernels: 57.4 us -> 50.9 us
    pallas_call x1, Pallas kernels: 54.8 us -> 49.4 us  [block_pass(): pl.pallas_call(lambda *refs: block_kernel(side, depth_z, divisor, *refs),...]
    pallas_call x1, Pallas kernels: 2.62 us -> 1.49 us  [finish_pass(): pl.pallas_call(finish_kernel, out_shape=(jax.ShapeDtypeStruct(grads.shape...]
where the time goes in v3:
time: 51.7 us; the launch traced here: 51.6 us
  Pallas kernels  50.9 us (98%)
  between operations  0.64 us (1%)
    pallas_call x1, Pallas kernels, block_pass(): pl.pallas_call(lambda *refs: block_kernel(side, depth_z, divisor, *refs),...  49.4 us
    pallas_call x1, Pallas kernels, finish_pass(): pl.pallas_call(finish_kernel, out_shape=(jax.ShapeDtypeStruct(grads.shape...  1.49 us

profile of v3, /device:TPU:1, one launch (start us, length us, event | category | flops | bytes accessed | tf_op | source)
XLA Modules:
  0.0 51.6 jit_solution(8372934205865240867)
XLA Ops:
  0.6 49.4 %conv_block.1 = (bf16[256,1536]{1,0:T(8,128)(2,1)S(1)}, f32[8,128]{1,0:T(8,128)S(1)}) custom-call(s32[4]{0:T(128)} %bitcast.8, s32[2]{0:T(128)} %bitcast.9, bf16[256,1536]{1,0:T(8,128)(2,1)} %bitcast.6, bf16[256,1536]{1,0:T(8,128)(2,1)} %bitcast.7, f32[31,1536]{1,0:T(8,128)} %refs_4_.1, f32[1536]{0:T(1024)} %refs_5_.1, f32[1536]{0:T(1024)} %refs_6_.1), custom_call_target="tpu_custom_call" | custom-call | tf_op jit(solution)/shard_map/conv_block/pallas_call | solution.py:337
  50.1 1.5 %finish.1 = (bf16[256,1536]{1,0:T(8,128)(2,1)}, f32[12,31]{1,0:T(8,128)}, f32[2,12]{1,0:T(2,128)}) custom-call(bf16[256,1536]{1,0:T(8,128)(2,1)S(1)} %get-tuple-element.8.grads, f32[8,128]{1,0:T(8,128)S(1)} %get-tuple-element.9.tile), custom_call_target="tpu_custom_call" | custom-call | tf_op jit(solution)/shard_map/finish/pallas_call | solution.py:396

commit v4 on v3

--- a/solution.py
+++ b/solution.py
@@ -15,6 +15,7 @@
 CORES = 2
 MOVES = 4
 PAIR = 2
+PARTS = 3
 MESH = pl.DeviceIdType.MESH
 
 
@@ -36,7 +37,7 @@
     side, depth_z, divisor,
     lengths, destination, features, cotangent, kernel, gain, bias,
     grad_out, tile_out,
-    stage, padded, conv, dnorm, dconv, owner, row_a, row_b, mean, scale, tap_sums, terms, columnwise, packed, grads,
+    stage, padded, conv, dnorm, dconv, spreading, row_a, row_b, mean, scale, tap_sums, terms, columnwise, packed, grads,
     from_core, sum_core, from_x, sum_x, from_y, sum_y, from_z,
     core_sent, core_got, x_sent, x_got, y_sent, y_got, z_sent, z_got, move_sent, move_got, stay_done,
 ):
@@ -78,35 +79,22 @@
     half_span = taps // 2
     blocks = channels // LANES
     spread = frames + GAP * (utterances - 1)
-    margin = GAP * (utterances - 1)
-    chunk = spread // 2
+    tiles = spread // TILE
+    marks = [TILE * ((tiles * c + PARTS - 1) // PARTS) for c in range(PARTS + 1)]
+    spans = [(marks[c], marks[c + 1] - marks[c]) for c in range(PARTS)]
     inverse = 1.0 / channels
 
-    place = lax.broadcasted_iota(jnp.int32, (spread, LANES), 0)
-    wide_owner = jnp.full((spread, LANES), -1, jnp.int32)
-    begin = 0
-    for u in range(utterances):
-        finish = begin + lengths[u]
-        here = (place >= begin + GAP * u) & (place < finish + GAP * u)
-        wide_owner = jnp.where(here, u, wide_owner)
-        begin = finish
-    owner[...] = wide_owner.astype(jnp.float32).astype(jnp.bfloat16)
+    frame = lax.broadcasted_iota(jnp.int32, (spread, frames), 1)
+    place = lax.broadcasted_iota(jnp.int32, (spread, frames), 0)
+    shift, finish = 0, 0
+    for u in range(utterances - 1):
+        finish = finish + lengths[u]
+        shift = shift + jnp.where(frame >= finish, GAP, 0)
+    spreading[...] = jnp.where(place == frame + shift, 1.0, 0.0).astype(jnp.bfloat16)
 
     edge = jnp.zeros((GAP, LANES), jnp.float32)
     terms[...] = jnp.zeros_like(terms)
 
-    def spread_rows(value):
-        ids = owner[...]
-        out = jnp.zeros((spread, LANES), value.dtype)
-        for u in range(utterances):
-            parts = [value]
-            if u > 0:
-                parts = [jnp.zeros((GAP * u, LANES), value.dtype)] + parts
-            if u < utterances - 1:
-                parts = parts + [jnp.zeros((margin - GAP * u, LANES), value.dtype)]
-            out = jnp.where(ids == u, jnp.concatenate(parts, axis=0), out)
-        return out.astype(jnp.float32)
-
     def columns(b):
         return pl.ds(pl.multiple_of(b * LANES, LANES), LANES)
 
@@ -114,19 +102,27 @@
         return jnp.broadcast_to(jnp.sum(ref[...], axis=1, keepdims=True), (spread, LANES))
 
     row_a[...] = jnp.zeros_like(row_a)
+
+    @pl.loop(0, blocks // PAIR)
+    def _(i):
+        part = pl.ds(pl.multiple_of(i * PAIR * LANES, PAIR * LANES), PAIR * LANES)
+        spread_features = jnp.dot(spreading[...], features[:, part], preferred_element_type=jnp.float32)
+        spread_cotangent = jnp.dot(spreading[...], cotangent[:, part], preferred_element_type=jnp.float32)
+        for r in range(PAIR):
+            padded[PAIR * i + r, pl.ds(GAP, spread), :] = spread_features[:, LANES * r : LANES * (r + 1)]
+            dnorm[PAIR * i + r] = spread_cotangent[:, LANES * r : LANES * (r + 1)]
 
     @pl.loop(0, blocks)
     def _(b):
         padded[b, pl.ds(0, GAP), :] = edge
         padded[b, pl.ds(GAP + spread, GAP), :] = edge
-        padded[b, pl.ds(GAP, spread), :] = spread_rows(features[:, columns(b)])
-        for c in range(2):
+        for begin, chunk in spans:
             value = convolve(
-                padded.at[b], GAP - half_span + chunk * c,
+                padded.at[b], GAP - half_span + begin,
                 lambda tap: kernel[pl.ds(tap, 1), columns(b)], taps, chunk,
             )
-            conv[b, pl.ds(chunk * c, chunk), :] = value
-            row_a[pl.ds(chunk * c, chunk), :] += value
+            conv[b, pl.ds(begin, chunk), :] = value
+            row_a[pl.ds(begin, chunk), :] += value
 
     mean[...] = row_total(row_a) * inverse
     row_a[...] = jnp.zeros_like(row_a)
@@ -148,7 +144,7 @@
         g = gain[columns(b)][None]
         act = normed * g + bias[columns(b)][None]
         gate = 0.5 * jnp.tanh(0.5 * act) + 0.5
-        dact = spread_rows(cotangent[:, columns(b)]) * gate * (1.0 + act * (1.0 - gate))
+        dact = dnorm[b] * gate * (1.0 + act * (1.0 - gate))
         terms[pl.ds(taps, 1), columns(b)] = jnp.sum(dact * normed, axis=0, keepdims=True)
         terms[pl.ds(taps + 1, 1), columns(b)] = jnp.sum(dact, axis=0, keepdims=True)
         weighted = dact * g
@@ -163,16 +159,16 @@
         dconv[b, pl.ds(0, GAP), :] = edge
         dconv[b, pl.ds(GAP + spread, GAP), :] = edge
         dconv[b, pl.ds(GAP, spread), :] = scale[...] * (dnorm[b] - mean[...] - conv[b] * row_b[...])
-        for c in range(2):
-            ours = dconv[b, pl.ds(GAP + chunk * c, chunk), :]
+        for begin, chunk in spans:
+            ours = dconv[b, pl.ds(GAP + begin, chunk), :]
             for group in tap_groups(taps):
                 window = padded[
-                    b, pl.ds(GAP - half_span + chunk * c + group[0], chunk + TILE * (len(group) - 1)), :
+                    b, pl.ds(GAP - half_span + begin + group[0], chunk + TILE * (len(group) - 1)), :
                 ]
                 for step, tap in enumerate(group):
                     product = ours * window[TILE * step : TILE * step + chunk]
                     part = jnp.sum(product.reshape(chunk // TILE, TILE, LANES), axis=0)
-                    tap_sums[tap] = part if c == 0 else tap_sums[tap] + part
+                    tap_sums[tap] = part if begin == 0 else tap_sums[tap] + part
         terms[pl.ds(0, taps), columns(b)] = jnp.sum(tap_sums[...], axis=1)
         square = jnp.concatenate([terms[:, columns(b)], jnp.zeros((LANES - KEEP, LANES), jnp.float32)], axis=0)
         columnwise[columns(b), :] = square.T
@@ -225,9 +221,9 @@
     size = frames // destination.shape[0]
 
     def input_gradient(b):
-        for c in range(2):
-            stage[pl.ds(chunk * c, chunk), :] = convolve(
-                dconv.at[b], GAP - half_span + chunk * c,
+        for begin, chunk in spans:
+            stage[pl.ds(begin, chunk), :] = convolve(
+                dconv.at[b], GAP - half_span + begin,
                 lambda tap: kernel[pl.ds(taps - 1 - tap, 1), columns(b)], taps, chunk,
             )
         spot = lax.broadcasted_iota(jnp.int32, (frames, LANES), 0)
@@ -348,7 +344,7 @@
             pltpu.VMEM((blocks, spread, LANES), f32),
             pltpu.VMEM((blocks, spread, LANES), f32),
             pltpu.VMEM((blocks, spread + 2 * GAP, LANES), f32),
-            pltpu.VMEM((spread, LANES), jnp.bfloat16),
+            pltpu.VMEM((spread, frames), jnp.bfloat16),
             pltpu.VMEM((spread, LANES), f32),
             pltpu.VMEM((spread, LANES), f32),
             pltpu.VMEM((spread, LANES), f32),

time: 51.7 us -> 50.6 us (0.979)
  Pallas kernels: 50.9 us -> 49.8 us
    pallas_call x1, Pallas kernels: 49.4 us -> 48.3 us  [block_pass(): pl.pallas_call(lambda *refs: block_kernel(side, depth_z, divisor, *refs),...]
where the time goes in v4:
time: 50.6 us; the launch traced here: 50.4 us
  Pallas kernels  49.8 us (98%)
  between operations  0.64 us (1%)
    pallas_call x1, Pallas kernels, block_pass(): pl.pallas_call(lambda *refs: block_kernel(side, depth_z, divisor, *refs),...  48.3 us
    pallas_call x1, Pallas kernels, finish_pass(): pl.pallas_call(finish_kernel, out_shape=(jax.ShapeDtypeStruct(grads.shape...  1.49 us

profile of v4, /device:TPU:1, one launch (start us, length us, event | category | flops | bytes accessed | tf_op | source)
XLA Modules:
  0.0 50.4 jit_solution(18094545871906481471)
XLA Ops:
  0.6 48.3 %conv_block.1 = (bf16[256,1536]{1,0:T(8,128)(2,1)S(1)}, f32[8,128]{1,0:T(8,128)S(1)}) custom-call(s32[4]{0:T(128)} %bitcast.8, s32[2]{0:T(128)} %bitcast.9, bf16[256,1536]{1,0:T(8,128)(2,1)} %bitcast.6, bf16[256,1536]{1,0:T(8,128)(2,1)} %bitcast.7, f32[31,1536]{1,0:T(8,128)} %refs_4_.1, f32[1536]{0:T(1024)} %refs_5_.1, f32[1536]{0:T(1024)} %refs_6_.1), custom_call_target="tpu_custom_call" | custom-call | tf_op jit(solution)/shard_map/conv_block/pallas_call | solution.py:333
  48.9 1.5 %finish.1 = (bf16[256,1536]{1,0:T(8,128)(2,1)}, f32[12,31]{1,0:T(8,128)}, f32[2,12]{1,0:T(2,128)}) custom-call(bf16[256,1536]{1,0:T(8,128)(2,1)S(1)} %get-tuple-element.8.grads, f32[8,128]{1,0:T(8,128)S(1)} %get-tuple-element.9.tile), custom_call_target="tpu_custom_call" | custom-call | tf_op jit(solution)/shard_map/finish/pallas_call | solution.py:392
